TPU v7x, 32 devices: a whole 2x2x4 slice. The times are simulated.
32 devices in a mesh: dp: 4 (over z), vocab: 8 (over y, x, core).
Axes of the slice: x: 2, y: 2, z: 4, core: 2. Of those that a mesh axis runs over, the one named last changes fastest.
Arguments:
- hidden: bfloat16 [4096, 4096], P(('dp', 'vocab')), may hold values from -4 to 4
- output_weight: bfloat16 [4096, 8192], P(None, 'vocab'), may hold values from -0.09375 to 0.09375
- owners: int32 [4096, 3], P(('dp', 'vocab')), may hold values from 0 to 7, all different within a row; in each aligned block of 128 rows (0 to 127, 128 to 255, ...) at most 64 rows name the same one
- negatives: int32 [4096, 3, 2], P(('dp', 'vocab')), may hold values from 0 to 7
- negative_mask: int32 [4096, 3, 2], P(('dp', 'vocab')), may hold values 0 or 1
- target_block: int32 [4096], P(('dp', 'vocab')), may hold values from 0 to 7
- target_word: int32 [4096], P(('dp', 'vocab')), may hold values from 0 to 127
- log_norm: bfloat16 [4096], P(('dp', 'vocab')), may hold values from 1 to 2
- cotangent: bfloat16 [4096], P(('dp', 'vocab')), may hold values from 4 to 8
Outputs:
- hidden_grad: bfloat16 [4096, 4096], P(('dp', 'vocab'))
- weight_grad: bfloat16 [4096, 8192], P('dp', 'vocab')
Inputs may be any that keep to these rules, and one draw needn't show every extreme that they name: Each row names 3 different owners; among the 128 rows of one device no owner is named by more than 64 rows, and in some device's rows an owner is named by exactly 64.
All inputs are finite; a program needn't handle non-finite values. No bound on the sum of `negative_mask` on one device may be relied on, other than what follows from the above.
Results may differ from a plain program's by a relative error of at most 0.015.
Values may be sent and summed in bfloat16 or wider, within the bound.
A program may use at most 128 MiB of HBM per device.

v0:
```python
import jax
import jax.numpy as jnp
from jax import lax
from jax.sharding import PartitionSpec as P

BLOCK = 128
BLK_DEV = 8
F32 = jnp.float32
BF16 = jnp.bfloat16


def body(
    hidden,
    output_weight,
    owners,
    negatives,
    negative_mask,
    target_block,
    target_word,
    log_norm,
    cotangent,
):
    tokens, width = hidden.shape
    visits = owners.shape[1]
    per_own = negatives.shape[2]
    n_vocab = lax.axis_size("vocab")
    n_dp = lax.axis_size("dp")
    me = lax.axis_index("vocab")
    my_dp = lax.axis_index("dp")
    words = output_weight.shape[1]
    capacity = max(2, tokens * visits * 4 // (3 * n_vocab))
    slots = n_vocab * capacity
    part = width // n_dp
    facts = jnp.concatenate(
        [
            owners.T,
            negatives.reshape(tokens, -1).T,
            negative_mask.reshape(tokens, -1).T,
            target_block[None, :],
            target_word[None, :],
        ],
        axis=0,
    ).astype(BF16)
    facts = jnp.concatenate([facts, log_norm[None, :], cotangent[None, :]], axis=0)
    facts = lax.all_gather(facts, ("dp", "vocab"), axis=0, tiled=False)
    blocks = n_dp * n_vocab
    group_rows = lax.all_gather(hidden, "vocab", axis=0, tiled=False)
    part_rows = lax.all_to_all(hidden, "dp", split_axis=1, concat_axis=0, tiled=True)
    part_rows = lax.all_gather(part_rows.reshape(n_dp, tokens, part), "vocab", axis=1)
    f = facts.astype(F32)
    pairs = visits * per_own
    hit = f[:, :visits, :] == me.astype(F32)
    neg = f[:, visits : visits + pairs, :]
    mask = f[:, visits + pairs : visits + 2 * pairs, :]
    base = visits + 2 * pairs
    t_block, t_word, norm, cot = (f[:, base + i, :] for i in range(4))
    named = jnp.any(hit, axis=1)
    cand = [jnp.where(hit[:, 0], t_block + 1.0, 0.0)]
    for n in range(per_own):
        value = jnp.zeros_like(t_block)
        for v in range(visits):
            i = v * per_own + n
            value = jnp.where(hit[:, v] & (mask[:, i] == 1.0), neg[:, i] + 1.0, value)
        cand.append(value)
    only = []
    for k, value in enumerate(cand):
        for earlier in cand[:k]:
            value = jnp.where(value == earlier, 0.0, value)
        only.append(value)
    upper = jnp.triu(jnp.ones((tokens, tokens), BF16), 1)
    rank = jnp.dot(named.astype(BF16), upper, preferred_element_type=F32)
    place = jnp.where(named, rank, -1.0)
    pick = (
        place[:, None, :] == jnp.arange(capacity, dtype=jnp.int32).astype(F32)[None, :, None]
    ).astype(BF16)
    attrs = jnp.stack(cand + only + [t_word, norm, cot], axis=1).astype(BF16)
    slot_facts = jnp.einsum("sct,sat->sca", pick, attrs, preferred_element_type=F32)
    kinds = per_own + 1
    all_only = slot_facts[:, :, kinds : 2 * kinds].reshape(n_dp * slots, kinds)
    mine = lax.dynamic_slice_in_dim(slot_facts, my_dp * n_vocab, n_vocab, 0).reshape(slots, -1)
    my_pick = lax.dynamic_slice_in_dim(pick, my_dp * n_vocab, n_vocab, 0)
    rows = jnp.einsum("sct,sth->sch", my_pick, group_rows, preferred_element_type=F32)
    rows = rows.astype(BF16).reshape(slots, width)
    scores = jnp.dot(rows, output_weight, preferred_element_type=F32)
    word_ids = jnp.arange(words, dtype=jnp.int32)[None, :]
    word_block = (word_ids // BLOCK + 1).astype(F32)
    word_in = (word_ids % BLOCK).astype(F32)
    counts = jnp.zeros((slots, words), F32)
    for k in range(kinds):
        counts = counts + jnp.where(mine[:, k : k + 1] == word_block, 1.0, 0.0)
    hot = jnp.where(
        (mine[:, 0:1] == word_block) & (mine[:, 2 * kinds : 2 * kinds + 1] == word_in), 1.0, 0.0
    )
    norm_col = mine[:, 2 * kinds + 1 : 2 * kinds + 2]
    cot_col = mine[:, 2 * kinds + 2 : 2 * kinds + 3]
    grown = jnp.where(counts > 0.0, counts * jnp.exp(scores - norm_col), 0.0)
    grad = (cot_col * (grown - hot)).astype(BF16)
    packed = []
    for k in range(kinds):
        which = mine[:, kinds + k : kinds + k + 1]
        value = jnp.zeros((slots, BLOCK), BF16)
        for b in range(BLK_DEV):
            value = jnp.where(which == b + 1.0, grad[:, b * BLOCK : (b + 1) * BLOCK], value)
        packed.append(value)
    packed = jnp.concatenate(packed, axis=1)
    packed = lax.all_gather(packed, "dp", axis=0, tiled=True)
    back = lax.dot_general(
        grad, output_weight, (((1,), (1,)), ((), ())), preferred_element_type=F32
    ).astype(BF16)
    back = jnp.einsum(
        "sct,sch->sth", my_pick, back.reshape(n_vocab, capacity, width), preferred_element_type=F32
    ).astype(BF16)
    hidden_grad = lax.psum_scatter(
        back.reshape(n_vocab * tokens, width), "vocab", scatter_dimension=0, tiled=True
    )
    part_slots = (
        jnp.einsum(
            "sct,sth->sch",
            pick,
            part_rows.reshape(blocks, tokens, part),
            preferred_element_type=F32,
        )
        .astype(BF16)
        .reshape(n_dp * slots, part)
    )
    spread = []
    for b in range(BLK_DEV):
        value = jnp.zeros((n_dp * slots, BLOCK), BF16)
        for k in range(kinds):
            value = jnp.where(
                all_only[:, k : k + 1] == b + 1.0, packed[:, k * BLOCK : (k + 1) * BLOCK], value
            )
        spread.append(value)
    spread = jnp.concatenate(spread, axis=1)
    weight_grad = lax.dot_general(
        part_slots, spread, (((0,), (0,)), ((), ())), preferred_element_type=F32
    ).astype(BF16)
    return (hidden_grad, weight_grad)


def solution(mesh):
    placed = (
        P(("dp", "vocab"), None),
        P(None, "vocab"),
        P(("dp", "vocab"), None),
        P(("dp", "vocab"), None, None),
        P(("dp", "vocab"), None, None),
        P(("dp", "vocab")),
        P(("dp", "vocab")),
        P(("dp", "vocab")),
        P(("dp", "vocab")),
    )
    return jax.shard_map(
        body,
        mesh=mesh,
        in_specs=placed,
        out_specs=(P(("dp", "vocab"), None), P("dp", "vocab")),
        check_vma=False,
    )
```

profile of v0, /device:TPU:0, one launch (start us, length us, event | category | flops | bytes accessed | tf_op | source)
XLA Modules:
  0.0 244.4 jit_solution(17321458530008942813)
XLA Ops:
  7.2 0.0 copy-start.2
  7.2 0.0 copy-start.3
  7.2 0.0 copy-start.5
  7.2 0.0 copy-start.6
  7.2 0.0 copy-start.4
  7.2 0.0 copy-start.7
  7.2 0.0 copy-start.8
  7.2 0.0 all-gather.10.cloned.1.call-start
  7.3 0.7 all-gather.10.cloned.1.call-update
  8.0 0.0 all-gather.12.cloned.1.call-start
  8.0 1.3 copy.20
  9.3 32.0 %all_to_all.16 = bf16[128,4,1024]{2,0,1:T(8,128)(2,1)} all-to-all(bf16[128,4,1024]{2,0,1:T(8,128)(2,1)S(1)} %bitcast.55), channel_id=1, replica_groups=mesh['dp'=4,'vocab'=8] {'dp'}, dimensions={1} | all-to-all | bytes 2097152 | tf_op jit(solution)/shard_map/all_to_all | solution.py:48
  41.3 0.0 all-gather.12.cloned.1.call-update
  41.3 0.0 all-gather.8.cloned.1.call-start
  41.4 0.0 copy-done.2
  41.4 0.0 copy-done.3
  41.5 0.0 copy-done.5
  41.5 0.0 copy-done.6
  41.5 0.0 copy-done.4
  41.5 0.0 copy-done.7
  41.5 0.0 copy-done.8
  41.5 0.2 concatenate.12
  41.7 40.7 %all-gather.3 = bf16[32,19,128]{2,1,0:T(8,128)(2,1)S(1)} all-gather(bf16[1,19,128]{2,1,0:T(8,128)(2,1)S(1)} %bitcast.56), channel_id=2, replica_groups=mesh['dp'=4,'vocab'=8] {'dp','vocab'}, dimensions={0}, use_global_device_ids=true | all-gather | bytes 160512 | tf_op jit(solution)/shard_map/all_gather | solution.py:45
  82.4 0.1 fusion.33
  82.5 0.3 fusion.17
  82.9 0.4 stack.4
  83.3 0.1 convolution_select_fusion
  83.4 0.5 fusion.3
  83.9 0.1 reshape.102
  84.0 0.1 compare_reduce_fusion.47
  84.2 0.2 broadcast_compare_fusion
  84.4 0.0 all-gather.10.cloned.1.call-done
  84.4 4.6 %convolution_convert_fusion.2 = bf16[8,64,4096]{2,1,0:T(8,128)(2,1)S(1)} fusion(bf16[8,128,4096]{2,1,0:T(8,128)(2,1)} %bitcast.48, pred[32,64,128]{2,1,0:T(32,128)(4,1)S(1)} %broadcast_compare_fusion, s32[]{:T(128)S(6)} %select_n.256), kind=kOutput, calls=%fused_computation.2 | convolution fusion | flops 538968064 | bytes 12648452 | tf_op jit(solution)/shard_map/sct,sth->sch/dot_general | solution.py:82
  89.1 8.7 %multiply_convert_fusion = bf16[512,1024]{1,0:T(8,128)(2,1)S(1)} fusion(bf16[512,4096]{1,0:T(8,128)(2,1)S(1)} %bitcast.49, bf16[4096,1024]{1,0:T(8,128)(2,1)} %param.10, f32[1024]{0:T(1024)S(1)} %get-tuple-element.78, f32[512]{0:T(512)S(1)} %bitcast.61, f32[1024]{0:T(1024)S(1)} %get-tuple-element.77, f32[512]{0:T(512)S(1)} %bitcast.64, f32[512]{0:T(512)S(1)} %bitcast.60, ...), kind=kOutput, calls=%fused_computation.8 | convolution fusion | flops 4304404480 | bytes 13651968 | tf_op jit(solution)/shard_map/dot_general | solution.py:84
  97.8 0.8 select_select_fusion
  98.5 0.8 select_select_fusion.1
  99.3 0.8 select_select_fusion.2
  100.1 0.8 pad_maximum_fusion
  100.9 0.0 all-gather.8.cloned.1.call-update
  100.9 0.2 reduce-scatter.2.cloned.1.call-start
  101.1 8.2 %convolution_convert_fusion.1 = bf16[512,4096]{1,0:T(8,128)(2,1)S(1)} fusion(bf16[512,1024]{1,0:T(8,128)(2,1)S(1)} %multiply_convert_fusion, bf16[4096,1024]{1,0:T(8,128)(2,1)} %param.10), kind=kOutput, calls=%fused_computation.1 | convolution fusion | flops 4297064448 | bytes 13631488 | tf_op jit(solution)/shard_map/dot_general | solution.py:107
  109.3 5.6 %convolution_convert_fusion = bf16[8,128,4096]{2,1,0:T(8,128)(2,1)} fusion(bf16[8,64,4096]{2,1,0:T(8,128)(2,1)S(1)} %bitcast.52, pred[32,64,128]{2,1,0:T(32,128)(4,1)S(1)} %broadcast_compare_fusion, s32[]{:T(128)S(6)} %select_n.256), kind=kOutput, calls=%fused_computation | convolution fusion | flops 541065216 | bytes 12648452 | tf_op jit(solution)/shard_map/sct,sch->sth/dot_general | solution.py:110
  114.9 0.0 reduce-scatter.2.cloned.1.call-update
  115.0 0.1 reshape.108
  115.1 0.6 compare_reduce_fusion.2
  115.7 8.7 %all-gather.12.cloned.1.call-done = bf16[4,1024,1024]{2,1,0:T(8,128)(2,1)} async-done(((bf16[4,128,1024]{2,1,0:T(8,128)(2,1)}), bf16[4,1024,1024]{2,1,0:T(8,128)(2,1)}) %all-gather.12.cloned.1.call-update) | async-done | bytes 8388624 | tf_op jit(solution)/shard_map/all_gather | solution.py:49
  124.4 6.6 %convolution_convert_fusion.3 = bf16[32,64,1024]{2,1,0:T(8,128)(2,1)} fusion(bf16[32,128,1024]{2,1,0:T(8,128)(2,1)} %bitcast.50, f32[32,128]{1,0:T(8,128)S(1)} %convolution_select_fusion, f32[64]{0:T(128)S(1)} %iota_convert_fusion), kind=kOutput, calls=%fused_computation.3 | convolution fusion | flops 539230208 | bytes 12599552 | tf_op jit(solution)/shard_map/sct,sth->sch/dot_general | solution.py:117
  131.0 32.6 %all-gather.8.cloned.1.call-done = bf16[2048,384]{1,0:T(8,128)(2,1)} async-done(((bf16[512,384]{1,0:T(8,128)(2,1)}), bf16[2048,384]{1,0:T(8,128)(2,1)}) %all-gather.8.cloned.1.call-update) | async-done | bytes 1572880 | tf_op jit(solution)/shard_map/all_gather | solution.py:106
  163.6 0.0 copy-start
  163.6 3.5 %select_dynamic-update-slice_fusion.7 = bf16[2048,1024]{1,0:T(8,128)(2,1)S(1)} fusion(pred[2048]{0:T(1024)(128)(4,1)S(1)} %get-tuple-element.58, pred[2048]{0:T(1024)(128)(4,1)S(1)} %get-tuple-element.57, pred[2048]{0:T(1024)(128)(4,1)S(1)} %get-tuple-element.56, bf16[2048,384]{1,0:T(8,128)(2,1)} %all-gather.8.cloned.1.call-done), kind=kLoop, calls=%fused_computation.22 | loop fusion | flops 786431 | bytes 2103296
  167.1 3.4 %select_dynamic-update-slice_fusion.6 = bf16[2048,1024]{1,0:T(8,128)(2,1)S(1)} fusion(bf16[2048,1024]{1,0:T(8,128)(2,1)S(1)} %select_dynamic-update-slice_fusion.7, pred[2048]{0:T(1024)(128)(4,1)S(1)} %get-tuple-element.16, pred[2048]{0:T(1024)(128)(4,1)S(1)} %get-tuple-element.9, pred[2048]{0:T(1024)(128)(4,1)S(1)} %get-tuple-element.3, ...), kind=kLoop, calls=%fused_computation.21 | loop fusion | flops 786432 | bytes 2103296
  170.5 0.0 copy-done
  170.5 1.8 select_dynamic-update-slice_fusion.5
  172.3 1.8 select_dynamic-update-slice_fusion.4
  174.1 0.0 copy-start.1
  174.1 1.8 select_dynamic-update-slice_fusion.3
  175.9 1.8 select_dynamic-update-slice_fusion.2
  177.6 1.8 select_dynamic-update-slice_fusion.1
  179.4 1.8 select_dynamic-update-slice_fusion
  181.2 0.0 copy-done.1
  181.2 5.7 %convolution_convert_fusion.4 = bf16[1024,1024]{1,0:T(8,128)(2,1)} fusion(bf16[2048,1024]{1,0:T(8,128)(2,1)S(1)} %bitcast.51, bf16[2048,1024]{1,0:T(8,128)(2,1)S(1)} %select_dynamic-update-slice_fusion), kind=kOutput, calls=%fused_computation.9 | convolution fusion | flops 4296015872 | bytes 10485760 | tf_op jit(solution)/shard_map/dot_general | solution.py:135
  187.0 50.9 %reduce-scatter.2.cloned.1.call-done = bf16[128,4096]{1,0:T(8,128)(2,1)} async-done(((bf16[1024,4096]{1,0:T(8,128)(2,1)}), bf16[128,4096]{1,0:T(8,128)(2,1)}) %reduce-scatter.2.cloned.1.call-update) | async-done | bytes 1048592 | tf_op jit(solution)/shard_map/reduce_scatter | solution.py:113
  (16 shorter events, 0.2 us)
Async XLA Ops:
  7.2 34.2 %copy-start.2 = (s32[128,3,2]{0,2,1:T(2,128)S(1)}, s32[128,3,2]{0,2,1:T(2,128)}, u32[]{:S(2)}) copy-start(s32[128,3,2]{0,2,1:T(2,128)} %param.12) | copy-start | bytes 9220
  7.2 34.3 %copy-start.3 = (s32[128,3,2]{0,2,1:T(2,128)S(1)}, s32[128,3,2]{0,2,1:T(2,128)}, u32[]{:S(2)}) copy-start(s32[128,3,2]{0,2,1:T(2,128)} %param.13) | copy-start | bytes 9220
  7.2 34.3 %copy-start.5 = (s32[128]{0:T(128)S(1)}, s32[128]{0:T(128)}, u32[]{:S(2)}) copy-start(s32[128]{0:T(128)} %param.15) | copy-start | bytes 1540
  7.2 34.3 %copy-start.6 = (s32[128]{0:T(128)S(1)}, s32[128]{0:T(128)}, u32[]{:S(2)}) copy-start(s32[128]{0:T(128)} %param.14) | copy-start | bytes 1540
  7.2 34.3 %copy-start.4 = (s32[128,3]{0,1:T(4,128)S(1)}, s32[128,3]{0,1:T(4,128)}, u32[]{:S(2)}) copy-start(s32[128,3]{0,1:T(4,128)} %param.11) | copy-start | bytes 4612
  7.2 34.3 %copy-start.7 = (bf16[128]{0:T(256)(128)(2,1)S(1)}, bf16[128]{0:T(256)(128)(2,1)}, u32[]{:S(2)}) copy-start(bf16[128]{0:T(256)(128)(2,1)} %param.16) | copy-start | bytes 772
  7.2 34.3 %copy-start.8 = (bf16[128]{0:T(256)(128)(2,1)S(1)}, bf16[128]{0:T(256)(128)(2,1)}, u32[]{:S(2)}) copy-start(bf16[128]{0:T(256)(128)(2,1)} %param.17) | copy-start | bytes 772
  7.2 77.2 %all-gather.10.cloned.1.call-start = ((), (), s32[]{:S(2)}) async-start(), calls=%async_computation.4 | async-start | bytes 9437184 | tf_op jit(solution)/shard_map/all_gather | solution.py:47
  8.0 116.4 %all-gather.12.cloned.1.call-start = ((), (), s32[]{:S(2)}) async-start(), calls=%async_computation.5 | async-start | bytes 9437184 | tf_op jit(solution)/shard_map/all_gather | solution.py:49
  41.3 122.3 %all-gather.8.cloned.1.call-start = ((), (), s32[]{:S(2)}) async-start(), calls=%async_computation.3 | async-start | bytes 1966080 | tf_op jit(solution)/shard_map/all_gather | solution.py:106
  100.9 137.0 %reduce-scatter.2.cloned.1.call-start = ((), (), s32[]{:S(2)}) async-start(), calls=%async_computation.2 | async-start | bytes 9437184 | tf_op jit(solution)/shard_map/reduce_scatter | solution.py:113
  163.6 6.9 %copy-start = (bf16[2048,384]{1,0:T(8,128)(2,1)S(1)}, bf16[2048,384]{1,0:T(8,128)(2,1)}, u32[]{:S(2)}) copy-start(bf16[2048,384]{1,0:T(8,128)(2,1)} %all-gather.8.cloned.1.call-done) | copy-start | bytes 4718596
  174.1 7.1 %copy-start.1 = (bf16[32,64,1024]{2,1,0:T(8,128)(2,1)S(1)}, bf16[32,64,1024]{2,1,0:T(8,128)(2,1)}, u32[]{:S(2)}) copy-start(bf16[32,64,1024]{2,1,0:T(8,128)(2,1)} %convolution_convert_fusion.3) | copy-start | bytes 12582916
Sparse Core Ops, SparseCore 0:
  9.9 58.0 all-gather.9
  70.0 54.3 all-gather.11
  126.5 37.0 all-gather.7
  167.5 70.3 reduce-scatter.1
where the time goes:
time: 245 us; the launch traced here: 244 us
  waiting for transfers between devices  93 us (38%)
  blocking collectives  72.6 us (30%)
  matrix products  40 us (16%)
  other arithmetic  22 us (9%)
  between operations  14.2 us (6%)
    reduce_scatter x1, waiting for transfers between devices, body(): lax.psum_scatter(back.reshape(n_vocab * tokens, width), 'vocab', scatter_...  50.9 us
    all_gather x1, blocking collectives, body(): facts = lax.all_gather(facts, ('dp', 'vocab'), axis=0, tiled=False)  40.7 us
    all_gather x1, waiting for transfers between devices, body(): packed = lax.all_gather(packed, 'dp', axis=0, tiled=True)  32.6 us
    all_to_all x1, blocking collectives, body(): lax.all_to_all(hidden, 'dp', split_axis=1, concat_axis=0, tiled=True)  32 us
    unnamed x7, other arithmetic  15.7 us
    all_gather x1, waiting for transfers between devices, body(): lax.all_gather(part_rows.reshape(n_dp, tokens, part), 'vocab', axis=1)  8.72 us
    dot_general x1, matrix products, body(): scores = jnp.dot(rows, output_weight, preferred_element_type=F32)  8.7 us
    dot_general x1, matrix products, body(): lax.dot_general(grad, output_weight, (((1,), (1,)), ((), ())), preferred_...  8.19 us
  transfers between devices with their start and end apart: 4, of which 3 were waited for; matrix products, arithmetic and copies ran while one was open for 26% of the time, Pallas kernels for 0%

commit v1 on v0

--- a/solution.py
+++ b/solution.py
@@ -103,7 +103,12 @@
             value = jnp.where(which == b + 1.0, grad[:, b * BLOCK : (b + 1) * BLOCK], value)
         packed.append(value)
     packed = jnp.concatenate(packed, axis=1)
-    packed = lax.all_gather(packed, "dp", axis=0, tiled=True)
+    ring = [packed]
+    for hop in range(3):
+        ring.append(lax.ppermute(ring[-1], "dp", [(dev, (dev + 1) % 4) for dev in range(4)]))
+    packed = jnp.roll(
+        jnp.concatenate(ring[::-1], axis=0), (lax.axis_index("dp") + 1) * ring[0].shape[0], axis=0
+    )
     back = lax.dot_general(
         grad, output_weight, (((1,), (1,)), ((), ())), preferred_element_type=F32
     ).astype(BF16)

time: 245 us -> 207 us (0.84)
  waiting for transfers between devices: 93 us -> 42.6 us
  other arithmetic: 22 us -> 37 us
  matrix products: 40 us -> 37.3 us
    reduce_scatter x1, waiting for transfers between devices: 50.9 us -> 5.71 us  [body(): lax.psum_scatter(back.reshape(n_vocab * tokens, width), 'vocab', scatter_...]
    ppermute x0 -> x3, waiting for transfers between devices: none -> 36.2 us  [body(): lax.ppermute(ring[-1], 'dp', [(dev, (dev + 1) % 4) for dev in range(4)])]
    all_gather x1 -> x0, waiting for transfers between devices: 32.6 us -> none  [body(): packed = lax.all_gather(packed, 'dp', axis=0, tiled=True)]
    unnamed x7 -> x9, other arithmetic: 15.7 us -> 28.9 us
    all_gather x1, waiting for transfers between devices: 8.72 us -> 0.01 us  [body(): lax.all_gather(part_rows.reshape(n_dp, tokens, part), 'vocab', axis=1)]
    dot_general x1, matrix products: 8.19 us -> 4.8 us  [body(): lax.dot_general(grad, output_weight, (((1,), (1,)), ((), ())), preferred_...]
    concatenate x1, other arithmetic: 1.77 us -> 4.25 us  [body(): spread = jnp.concatenate(spread, axis=1)]
  transfers between devices with their start and end apart: 4 -> 6, of which waited for: 3 -> 4; matrix products, arithmetic and copies ran while one was open for 26% -> 37% of each run, Pallas kernels for 0% -> 0%
where the time goes in v1:
time: 207 us; the launch traced here: 206 us
  blocking collectives  72.6 us (35%)
  waiting for transfers between devices  42.6 us (21%)
  matrix products  37.3 us (18%)
  other arithmetic  37 us (18%)
  between operations  14.2 us (7%)
  local copies, waits for them, and re-layouts  2.55 us (1%)
    all_gather x1, blocking collectives, body(): facts = lax.all_gather(facts, ('dp', 'vocab'), axis=0, tiled=False)  40.7 us
    ppermute x3, waiting for transfers between devices, body(): lax.ppermute(ring[-1], 'dp', [(dev, (dev + 1) % 4) for dev in range(4)])  36.2 us
    all_to_all x1, blocking collectives, body(): lax.all_to_all(hidden, 'dp', split_axis=1, concat_axis=0, tiled=True)  32 us
    unnamed x9, other arithmetic  28.9 us
    dot_general x1, matrix products, body(): scores = jnp.dot(rows, output_weight, preferred_element_type=F32)  8.85 us
    dot_general x1, matrix products, body(): lax.dot_general(part_slots, spread, (((0,), (0,)), ((), ())), preferred_e...  7.99 us
    reduce_scatter x1, waiting for transfers between devices, body(): lax.psum_scatter(back.reshape(n_vocab * tokens, width), 'vocab', scatter_...  5.71 us
    dot_general x1, matrix products, body(): jnp.einsum('sct,sch->sth', my_pick, back.reshape(n_vocab, capacity, width...  5.59 us
  transfers between devices with their start and end apart: 6, of which 4 were waited for; matrix products, arithmetic and copies ran while one was open for 37% of the time, Pallas kernels for 0%

profile of v1, /device:TPU:0, one launch (start us, length us, event | category | flops | bytes accessed | tf_op | source)
XLA Modules:
  0.0 206.5 jit_solution(4912916859288794732)
XLA Ops:
  7.2 0.0 copy-start.1
  7.2 0.0 copy-start.2
  7.2 0.0 copy-start.4
  7.2 0.0 copy-start.5
  7.2 0.0 copy-start.3
  7.2 0.0 copy-start.6
  7.2 0.0 all-gather.7.cloned.1.call-start
  7.3 0.7 all-gather.7.cloned.1.call-update
  8.0 0.0 all-gather.9.cloned.1.call-start
  8.0 1.3 copy.20
  9.3 32.0 %all_to_all.16 = bf16[128,4,1024]{2,0,1:T(8,128)(2,1)} all-to-all(bf16[128,4,1024]{2,0,1:T(8,128)(2,1)S(1)} %bitcast.55), channel_id=1, replica_groups=mesh['dp'=4,'vocab'=8] {'dp'}, dimensions={1} | all-to-all | bytes 2097152 | tf_op jit(solution)/shard_map/all_to_all | solution.py:48
  41.3 0.0 all-gather.9.cloned.1.call-update
  41.3 0.0 reduce-scatter.2.cloned.1.call-start
  41.5 0.0 copy-done.5
  41.5 0.0 copy-done.6
  41.5 0.0 copy-done.7
  41.5 0.2 concatenate.18
  41.7 40.7 %all-gather.3 = bf16[32,19,128]{2,1,0:T(8,128)(2,1)S(1)} all-gather(bf16[1,19,128]{2,1,0:T(8,128)(2,1)S(1)} %bitcast.56), channel_id=2, replica_groups=mesh['dp'=4,'vocab'=8] {'dp','vocab'}, dimensions={0}, use_global_device_ids=true | all-gather | bytes 160512 | tf_op jit(solution)/shard_map/all_gather | solution.py:45
  82.4 0.1 fusion.33
  82.5 0.3 fusion.17
  82.9 0.4 stack.4
  83.3 0.1 convolution_select_fusion
  83.4 0.5 fusion.3
  83.9 0.1 reshape.102
  84.0 0.2 broadcast_compare_fusion
  84.2 0.0 all-gather.7.cloned.1.call-done
  84.3 0.0 slice-start
  84.3 4.8 %convolution_convert_fusion.2 = bf16[8,64,4096]{2,1,0:T(8,128)(2,1)S(1)} fusion(bf16[8,128,4096]{2,1,0:T(8,128)(2,1)} %bitcast.48, pred[32,64,128]{2,1,0:T(32,128)(4,1)S(1)} %broadcast_compare_fusion, s32[]{:T(128)S(6)} %select_n.268), kind=kOutput, calls=%fused_computation.2 | convolution fusion | flops 538968064 | bytes 12648452 | tf_op jit(solution)/shard_map/sct,sth->sch/dot_general | solution.py:82
  89.1 0.0 slice-start.1
  89.1 8.8 %multiply_convert_fusion = bf16[512,1024]{1,0:T(8,128)(2,1)S(1)} fusion(bf16[512,4096]{1,0:T(8,128)(2,1)S(1)} %bitcast.49, bf16[4096,1024]{1,0:T(8,128)(2,1)} %param.10, f32[1024]{0:T(1024)S(1)} %get-tuple-element.78, f32[512]{0:T(512)S(1)} %bitcast.61, f32[1024]{0:T(1024)S(1)} %get-tuple-element.77, f32[512]{0:T(512)S(1)} %bitcast.64, f32[512]{0:T(512)S(1)} %bitcast.60, ...), kind=kOutput, calls=%fused_computation.8 | convolution fusion | flops 4304404480 | bytes 13651968 | tf_op jit(solution)/shard_map/dot_general | solution.py:84
  98.0 4.8 %convolution_convert_fusion.1 = bf16[512,4096]{1,0:T(8,128)(2,1)S(1)} fusion(bf16[512,1024]{1,0:T(8,128)(2,1)S(1)} %multiply_convert_fusion, bf16[4096,1024]{1,0:T(8,128)(2,1)S(1)} %bitcast.68), kind=kOutput, calls=%fused_computation.1 | convolution fusion | flops 4297064448 | bytes 13631488 | tf_op jit(solution)/shard_map/dot_general | solution.py:112
  102.8 5.6 %convolution_convert_fusion = bf16[8,128,4096]{2,1,0:T(8,128)(2,1)} fusion(bf16[8,64,4096]{2,1,0:T(8,128)(2,1)S(1)} %bitcast.52, pred[32,64,128]{2,1,0:T(32,128)(4,1)S(1)} %broadcast_compare_fusion, s32[]{:T(128)S(6)} %select_n.268), kind=kOutput, calls=%fused_computation | convolution fusion | flops 541065216 | bytes 12648452 | tf_op jit(solution)/shard_map/sct,sch->sth/dot_general | solution.py:115
  108.4 0.0 reduce-scatter.2.cloned.1.call-update
  108.4 0.2 compare_reduce_fusion.47
  108.5 0.8 select_select_fusion
  109.3 0.8 select_select_fusion.1
  110.1 0.8 select_select_fusion.2
  110.9 0.1 pad_maximum_fusion
  110.9 0.1 collective-permute-start
  111.0 13.1 %collective-permute-done = bf16[512,384]{1,0:T(8,128)(2,1)S(1)} collective-permute-done((bf16[512,384]{1,0:T(8,128)(2,1)S(1)}, bf16[512,384]{1,0:T(8,128)(2,1)S(1)}, u32[]{:S(2)}, u32[]{:S(2)}) %collective-permute-start) | collective-permute-done | bytes 393248 | tf_op jit(solution)/shard_map/ppermute | solution.py:108
  124.1 0.0 collective-permute-start.1
  124.1 12.3 %collective-permute-done.1 = bf16[512,384]{1,0:T(8,128)(2,1)S(1)} collective-permute-done((bf16[512,384]{1,0:T(8,128)(2,1)S(1)}, bf16[512,384]{1,0:T(8,128)(2,1)S(1)}, u32[]{:S(2)}, u32[]{:S(2)}) %collective-permute-start.1) | collective-permute-done | bytes 393248 | tf_op jit(solution)/shard_map/ppermute | solution.py:108
  136.4 0.0 collective-permute-start.2
  136.5 0.1 reshape.108
  136.6 0.6 compare_reduce_fusion.2
  137.2 10.7 %collective-permute-done.2 = bf16[512,384]{1,0:T(8,128)(2,1)S(1)} collective-permute-done((bf16[512,384]{1,0:T(8,128)(2,1)S(1)}, bf16[512,384]{1,0:T(8,128)(2,1)S(1)}, u32[]{:S(2)}, u32[]{:S(2)}) %collective-permute-start.2) | collective-permute-done | bytes 393248 | tf_op jit(solution)/shard_map/ppermute | solution.py:108
  147.9 0.1 constant_dynamic-update-slice_fusion.6
  148.0 0.1 constant_dynamic-update-slice_fusion.5
  148.1 0.1 constant_dynamic-update-slice_fusion.4
  148.2 0.1 constant_dynamic-update-slice_fusion.3
  148.2 0.1 constant_dynamic-update-slice_fusion.2
  148.3 0.1 constant_dynamic-update-slice_fusion.1
  148.4 0.1 constant_dynamic-update-slice_fusion
  148.5 3.0 %select_dynamic-update-slice_fusion.7 = bf16[2048,1024]{1,0:T(8,128)(2,1)} fusion(pred[2048]{0:T(1024)(128)(4,1)S(1)} %get-tuple-element.58, pred[2048]{0:T(1024)(128)(4,1)S(1)} %get-tuple-element.57, pred[2048]{0:T(1024)(128)(4,1)S(1)} %get-tuple-element.56, bf16[4096,384]{1,0:T(8,128)(2,1)S(1)} %constant_dynamic-update-slice_fusion, s32[]{:T(128)S(6)} %select_n.311, ...), kind=kLoop, calls=%fused_computation.22 | loop fusion | flops 786431 | bytes 2103308
  151.5 4.4 %select_dynamic-update-slice_fusion.6 = bf16[2048,1024]{1,0:T(8,128)(2,1)} fusion(bf16[2048,1024]{1,0:T(8,128)(2,1)} %select_dynamic-update-slice_fusion.7, pred[2048]{0:T(1024)(128)(4,1)S(1)} %get-tuple-element.16, pred[2048]{0:T(1024)(128)(4,1)S(1)} %get-tuple-element.9, pred[2048]{0:T(1024)(128)(4,1)S(1)} %get-tuple-element.3, ...), kind=kLoop, calls=%fused_computation.21 | loop fusion | flops 786432 | bytes 2103308
  155.9 4.2 %select_dynamic-update-slice_fusion.5 = bf16[2048,1024]{1,0:T(8,128)(2,1)} fusion(bf16[2048,1024]{1,0:T(8,128)(2,1)} %select_dynamic-update-slice_fusion.6, pred[2048]{0:T(1024)(128)(4,1)S(1)} %get-tuple-element.17, pred[2048]{0:T(1024)(128)(4,1)S(1)} %get-tuple-element.10, pred[2048]{0:T(1024)(128)(4,1)S(1)} %get-tuple-element.4, ...), kind=kLoop, calls=%fused_computation.20 | loop fusion | flops 786432 | bytes 2103308
  160.1 4.4 %select_dynamic-update-slice_fusion.4 = bf16[2048,1024]{1,0:T(8,128)(2,1)} fusion(bf16[2048,1024]{1,0:T(8,128)(2,1)} %select_dynamic-update-slice_fusion.5, pred[2048]{0:T(1024)(128)(4,1)S(1)} %get-tuple-element.18, pred[2048]{0:T(1024)(128)(4,1)S(1)} %get-tuple-element.11, pred[2048]{0:T(1024)(128)(4,1)S(1)} %get-tuple-element.5, ...), kind=kLoop, calls=%fused_computation.19 | loop fusion | flops 786432 | bytes 2103308
  164.5 4.2 %select_dynamic-update-slice_fusion.3 = bf16[2048,1024]{1,0:T(8,128)(2,1)} fusion(bf16[2048,1024]{1,0:T(8,128)(2,1)} %select_dynamic-update-slice_fusion.4, pred[2048]{0:T(1024)(128)(4,1)S(1)} %get-tuple-element.19, pred[2048]{0:T(1024)(128)(4,1)S(1)} %get-tuple-element.12, pred[2048]{0:T(1024)(128)(4,1)S(1)} %get-tuple-element.6, ...), kind=kLoop, calls=%fused_computation.18 | loop fusion | flops 786432 | bytes 2103308
  168.7 4.3 %select_dynamic-update-slice_fusion.2 = bf16[2048,1024]{1,0:T(8,128)(2,1)} fusion(bf16[2048,1024]{1,0:T(8,128)(2,1)} %select_dynamic-update-slice_fusion.3, pred[2048]{0:T(1024)(128)(4,1)S(1)} %get-tuple-element.20, pred[2048]{0:T(1024)(128)(4,1)S(1)} %get-tuple-element.13, pred[2048]{0:T(1024)(128)(4,1)S(1)} %get-tuple-element.7, ...), kind=kLoop, calls=%fused_computation.17 | loop fusion | flops 786432 | bytes 2103308
  173.1 4.3 %select_dynamic-update-slice_fusion.1 = bf16[2048,1024]{1,0:T(8,128)(2,1)} fusion(bf16[2048,1024]{1,0:T(8,128)(2,1)} %select_dynamic-update-slice_fusion.2, pred[2048]{0:T(1024)(128)(4,1)S(1)} %get-tuple-element.59, pred[2048]{0:T(1024)(128)(4,1)S(1)} %get-tuple-element.14, pred[2048]{0:T(1024)(128)(4,1)S(1)} %get-tuple-element.8, ...), kind=kLoop, calls=%fused_computation.16 | loop fusion | flops 786432 | bytes 2103308
  177.3 4.2 %select_dynamic-update-slice_fusion = bf16[2048,1024]{1,0:T(8,128)(2,1)} fusion(bf16[2048,1024]{1,0:T(8,128)(2,1)} %select_dynamic-update-slice_fusion.1, pred[2048]{0:T(1024)(128)(4,1)S(1)} %get-tuple-element.60, pred[2048]{0:T(1024)(128)(4,1)S(1)} %get-tuple-element.15, pred[2048]{0:T(1024)(128)(4,1)S(1)} %get-tuple-element.2, ...), kind=kLoop, calls=%fused_computation.15 | loop fusion | flops 786432 | bytes 2103308 | tf_op jit(solution)/shard_map/concatenate | solution.py:139
  181.6 4.7 %convolution_convert_fusion.3 = bf16[32,64,1024]{2,1,0:T(8,128)(2,1)S(1)} fusion(bf16[32,128,1024]{2,1,0:T(8,128)(2,1)} %bitcast.50, f32[32,128]{1,0:T(8,128)S(1)} %convolution_select_fusion, f32[64]{0:T(128)S(1)} %iota_convert_fusion), kind=kOutput, calls=%fused_computation.3 | convolution fusion | flops 539230208 | bytes 12599552 | tf_op jit(solution)/shard_map/sct,sth->sch/dot_general | solution.py:122
  186.3 8.0 %convolution_convert_fusion.4 = bf16[1024,1024]{1,0:T(8,128)(2,1)} fusion(bf16[2048,1024]{1,0:T(8,128)(2,1)S(1)} %bitcast.51, bf16[2048,1024]{1,0:T(8,128)(2,1)} %select_dynamic-update-slice_fusion), kind=kOutput, calls=%fused_computation.9 | convolution fusion | flops 4296015872 | bytes 10485760 | tf_op jit(solution)/shard_map/dot_general | solution.py:140
  194.2 5.7 %reduce-scatter.2.cloned.1.call-done = bf16[128,4096]{1,0:T(8,128)(2,1)} async-done(((bf16[1024,4096]{1,0:T(8,128)(2,1)}), bf16[128,4096]{1,0:T(8,128)(2,1)}) %reduce-scatter.2.cloned.1.call-update) | async-done | bytes 1048592 | tf_op jit(solution)/shard_map/reduce_scatter | solution.py:118
  (28 shorter events, 0.3 us)
Async XLA Ops:
  7.2 34.2 %copy-start.1 = (s32[128,3,2]{0,2,1:T(2,128)S(1)}, s32[128,3,2]{0,2,1:T(2,128)}, u32[]{:S(2)}) copy-start(s32[128,3,2]{0,2,1:T(2,128)} %param.12) | copy-start | bytes 9220
  7.2 34.3 %copy-start.2 = (s32[128,3,2]{0,2,1:T(2,128)S(1)}, s32[128,3,2]{0,2,1:T(2,128)}, u32[]{:S(2)}) copy-start(s32[128,3,2]{0,2,1:T(2,128)} %param.13) | copy-start | bytes 9220
  7.2 34.3 %copy-start.4 = (s32[128]{0:T(128)S(1)}, s32[128]{0:T(128)}, u32[]{:S(2)}) copy-start(s32[128]{0:T(128)} %param.15) | copy-start | bytes 1540
  7.2 34.3 %copy-start.5 = (s32[128]{0:T(128)S(1)}, s32[128]{0:T(128)}, u32[]{:S(2)}) copy-start(s32[128]{0:T(128)} %param.14) | copy-start | bytes 1540
  7.2 34.3 %copy-start.3 = (s32[128,3]{0,1:T(4,128)S(1)}, s32[128,3]{0,1:T(4,128)}, u32[]{:S(2)}) copy-start(s32[128,3]{0,1:T(4,128)} %param.11) | copy-start | bytes 4612
  7.2 34.3 %copy-start.6 = (bf16[128]{0:T(256)(128)(2,1)S(1)}, bf16[128]{0:T(256)(128)(2,1)}, u32[]{:S(2)}) copy-start(bf16[128]{0:T(256)(128)(2,1)} %param.16) | copy-start | bytes 772
  7.2 34.3 %copy-start.7 = (bf16[128]{0:T(256)(128)(2,1)S(1)}, bf16[128]{0:T(256)(128)(2,1)}, u32[]{:S(2)}) copy-start(bf16[128]{0:T(256)(128)(2,1)} %param.17) | copy-start | bytes 772
  7.2 77.0 %all-gather.7.cloned.1.call-start = ((), (), s32[]{:S(2)}) async-start(), calls=%async_computation.3 | async-start | bytes 9437184 | tf_op jit(solution)/shard_map/all_gather | solution.py:47
  8.0 173.6 %all-gather.9.cloned.1.call-start = ((), (), s32[]{:S(2)}) async-start(), calls=%async_computation.4 | async-start | bytes 9437184 | tf_op jit(solution)/shard_map/all_gather | solution.py:49
  41.3 158.6 %reduce-scatter.2.cloned.1.call-start = ((), (), s32[]{:S(2)}) async-start(), calls=%async_computation.2 | async-start | bytes 9437184 | tf_op jit(solution)/shard_map/reduce_scatter | solution.py:118
  84.3 13.7 %slice-start = ((s8[8388608]{0:T(1024)(128)(4,1)}), s8[4194304]{0:T(1024)(128)(4,1)S(1)}, s32[]{:S(2)}) async-start(s8[8388608]{0:T(1024)(128)(4,1)} %bitcast.67), calls=%async_computation.5 | async-start | bytes 8388608
  89.1 8.9 %slice-start.1 = ((s8[8388608]{0:T(1024)(128)(4,1)}), s8[4194304]{0:T(1024)(128)(4,1)S(1)}, s32[]{:S(2)}) async-start(s8[8388608]{0:T(1024)(128)(4,1)} %bitcast.67), calls=%async_computation.6 | async-start | bytes 8388608
  110.9 13.2 %collective-permute-start = (bf16[512,384]{1,0:T(8,128)(2,1)S(1)}, bf16[512,384]{1,0:T(8,128)(2,1)S(1)}, u32[]{:S(2)}, u32[]{:S(2)}) collective-permute-start(bf16[512,384]{1,0:T(8,128)(2,1)S(1)} %pad_maximum_fusion), channel_id=1, source_target_pairs={{0,8},{8,16},{16,24},{24,0},{1,9},{9,17},{17,25},{25,1},{2,10},{10... | collective-permute-start | bytes 1179656 | tf_op jit(solution)/shard_map/ppermute | solution.py:108
  124.1 12.3 %collective-permute-start.1 = (bf16[512,384]{1,0:T(8,128)(2,1)S(1)}, bf16[512,384]{1,0:T(8,128)(2,1)S(1)}, u32[]{:S(2)}, u32[]{:S(2)}) collective-permute-start(bf16[512,384]{1,0:T(8,128)(2,1)S(1)} %collective-permute-done), channel_id=1, source_target_pairs={{0,8},{8,16},{16,24},{24,0},{1,9},{9,17},{17,25},{25,1},{2,10},{10... | collective-permute-start | bytes 1179656 | tf_op jit(solution)/shard_map/ppermute | solution.py:108
  136.4 11.4 %collective-permute-start.2 = (bf16[512,384]{1,0:T(8,128)(2,1)S(1)}, bf16[512,384]{1,0:T(8,128)(2,1)S(1)}, u32[]{:S(2)}, u32[]{:S(2)}) collective-permute-start(bf16[512,384]{1,0:T(8,128)(2,1)S(1)} %collective-permute-done.1), channel_id=1, source_target_pairs={{0,8},{8,16},{16,24},{24,0},{1,9},{9,17},{17,25},{25,1},{2,10},{10... | collective-permute-start | bytes 1179656 | tf_op jit(solution)/shard_map/ppermute | solution.py:108
  148.5 3.0 %copy-start = (bf16[4096,384]{1,0:T(8,128)(2,1)}, bf16[4096,384]{1,0:T(8,128)(2,1)S(1)}, u32[]{:S(2)}) copy-start(bf16[4096,384]{1,0:T(8,128)(2,1)S(1)} %constant_dynamic-update-slice_fusion) | copy-start | bytes 9437188
Sparse Core Ops, SparseCore 0:
  9.9 58.0 all-gather.6
  70.0 54.3 all-gather.8
  128.4 71.4 reduce-scatter.1
